TPU v7x, 32 devices: a whole 2x2x4 slice. The times are simulated.
32 devices in a mesh: dp: 4 (over x, core), fsdp: 2 (over y), enc: 4 (over z).
Axes of the slice: x: 2, y: 2, z: 4, core: 2. Of those that a mesh axis runs over, the one named last changes fastest.
Arguments:
- hidden: bfloat16 [8192, 8192], P(('dp', 'fsdp', 'enc')), may hold values from -40 to 40
- residual_gradient: bfloat16 [8192, 8192], P(('dp', 'fsdp', 'enc')), may hold values from -3 to 3
- value_output_gradient: bfloat16 [8192, 1024], P(('dp', 'fsdp', 'enc')), may hold values from -6 to 6
- attention_norm_gain: float32 [8192], replicated, may hold values from 0.1 to 1.9
- value_frozen_weight: bfloat16 [8192, 1024], P('fsdp'), may hold values from -0.0625 to 0.0625
- value_down_factor: bfloat16 [8192, 16], replicated, may hold values from -0.0625 to 0.0625
- value_up_factor: bfloat16 [16, 1024], replicated, may hold values from -0.29882812 to 0.29882812
- merger_frozen_weight: bfloat16 [5120, 8192], P(None, ('fsdp', 'enc')), may hold values from -0.078125 to 0.078125
- merger_down_factor: bfloat16 [5120, 16], replicated, may hold values from -0.078125 to 0.078125
- merger_up_factor: bfloat16 [16, 8192], P(None, ('fsdp', 'enc')), may hold values from -0.29882812 to 0.29882812
- merger_saved_preactivation: bfloat16 [1024, 5120], P(('dp', 'fsdp', 'enc')), may hold values from -5 to 5
- image_token_counts: int32 [32], P('dp'), may hold values from 8 to 16, as said below
- image_encoder_owner: int32 [32], P('dp'), may hold values from 0 to 7, as said below
- image_first_rows: int32 [32], P(('dp', 'fsdp', 'enc')), may hold values from 0 to 255, as said below
Outputs:
- layer_input_gradient: bfloat16 [8192, 8192], P(('dp', 'fsdp', 'enc'))
- preactivation_gradient: bfloat16 [1024, 5120], P(('dp', 'fsdp', 'enc'))
- value_down_gradient: float32 [8192, 16], replicated
- value_up_gradient: float32 [16, 1024], replicated
- merger_down_gradient: float32 [5120, 16], replicated
- merger_up_gradient: float32 [16, 8192], P(None, ('fsdp', 'enc'))
Inputs may be any that keep to these rules, and one draw needn't show every extreme that they name: `image_token_counts`: within each data replica some encoder device owns exactly 2 images, all of 16 visual tokens, so its rows fill all 32; no other device owns more than 2 images. `image_encoder_owner`: encoder devices are numbered within the data replica in mesh order. `image_first_rows`: images of one device lie inside its 256 rows in increasing order and don't intersect.
All inputs are finite; a program needn't handle non-finite values.
Results may differ from a plain program's by a relative error of at most 0.0085.
Values may be sent and summed in bfloat16 or wider, within the bound.
No kernel may reach another device: no remote copies, remote signals or barrier semaphores. Data moves between devices by JAX's collectives and lax.ppermute only.
A program may use at most 192 MiB of HBM per device.

v0:
```python
import jax
import jax.numpy as jnp
from jax import lax
from jax.sharding import PartitionSpec as P

MAXIMG = 16
adapter_scale = 2.0
norm_eps = 1e-06


def gelu_parts(preact):
    normal_cdf = 0.5 * (1.0 + lax.erf(preact * 0.7071067811865476))
    normal_pdf = jnp.exp(-0.5 * preact * preact) * 0.3989422804014327
    return (normal_cdf, normal_pdf)


def owner_layout(image_token_counts, image_encoder_owner, owner_count, owner_room, slot_len):
    total_images = image_token_counts.shape[0]
    image_ids = jnp.arange(total_images)
    same_owner = image_encoder_owner[:, None] == image_encoder_owner[None, :]
    earlier = image_ids[None, :] < image_ids[:, None]
    starts = jnp.sum(jnp.where(same_owner & earlier, image_token_counts[None, :], 0), axis=1)
    row_index = jnp.arange(owner_count * owner_room)
    row_owner = row_index // owner_room
    row_place = row_index % owner_room
    matches = (
        (row_owner[:, None] == image_encoder_owner[None, :])
        & (row_place[:, None] >= starts[None, :])
        & (row_place[:, None] < (starts + image_token_counts)[None, :])
    )
    source = jnp.sum(
        jnp.where(matches, image_ids[None, :] * slot_len + row_place[:, None] - starts[None, :], 0),
        axis=1,
    )
    valid_rows = jnp.any(matches, axis=1)
    return (source, valid_rows)


def take_slots(layer_input_gradient, counts_in, offsets_in):
    padded = jnp.concatenate(
        [
            layer_input_gradient,
            jnp.zeros((MAXIMG, layer_input_gradient.shape[1]), layer_input_gradient.dtype),
        ],
        axis=0,
    )
    window = lax.dynamic_slice_in_dim(padded, offsets_in[0], MAXIMG, 0)
    inside = jnp.arange(MAXIMG) < counts_in[0]
    pieces = jnp.where(inside[:, None], window, jnp.zeros_like(window))
    return pieces


def decoder_layer_block(
    incoming_rows,
    residual_input,
    value_incoming,
    attention_norm_gain,
    passed_gradient,
    value_down_factor,
    value_up_factor,
):
    values = incoming_rows.astype(jnp.float32)
    inverse = lax.rsqrt(jnp.mean(values * values, axis=1, keepdims=True) + norm_eps)
    normalized_input = (values * inverse * attention_norm_gain).astype(jnp.bfloat16)
    value_low_product = jnp.dot(
        value_incoming, value_up_factor.T, preferred_element_type=jnp.float32
    ).astype(jnp.bfloat16)
    normalized_gradient = passed_gradient.astype(jnp.float32) + adapter_scale * jnp.dot(
        value_low_product, value_down_factor.T, preferred_element_type=jnp.float32
    )
    gained = attention_norm_gain * normalized_gradient
    layer_input_gradient = (
        residual_input.astype(jnp.float32)
        + inverse * gained
        - values * inverse**3 * jnp.mean(values * gained, axis=1, keepdims=True)
    ).astype(jnp.bfloat16)
    projected_rows = jnp.dot(
        normalized_input, value_down_factor, preferred_element_type=jnp.float32
    ).astype(jnp.bfloat16)
    up_term = lax.dot_general(
        projected_rows, value_incoming, (((0,), (0,)), ((), ())), preferred_element_type=jnp.float32
    )
    down_term = lax.dot_general(
        normalized_input,
        value_low_product,
        (((0,), (0,)), ((), ())),
        preferred_element_type=jnp.float32,
    )
    return (layer_input_gradient, down_term, up_term)


def body(
    hidden,
    residual_gradient,
    value_output_gradient,
    attention_norm_gain,
    value_frozen_weight,
    value_down_factor,
    value_up_factor,
    merger_frozen_weight,
    merger_down_factor,
    merger_up_factor,
    merger_saved_preactivation,
    image_token_counts,
    image_encoder_owner,
    image_first_rows,
):
    device_total = lax.axis_size("dp") * lax.axis_size("fsdp") * lax.axis_size("enc")
    gradient_scale = 256.0 / (hidden.shape[0] * device_total)
    scale_factor = gradient_scale * adapter_scale
    owner_count = lax.axis_size("fsdp") * lax.axis_size("enc")
    owner_room = merger_saved_preactivation.shape[0]
    preact = merger_saved_preactivation.astype(jnp.float32)
    normal_cdf, normal_pdf = gelu_parts(preact)
    activation = (preact * normal_cdf).astype(jnp.bfloat16)
    act_low = jnp.dot(activation, merger_down_factor, preferred_element_type=jnp.float32).astype(
        jnp.bfloat16
    )
    all_low = lax.all_gather(act_low, ("fsdp", "enc"), axis=0, tiled=True)
    columns = lax.dot_general(
        lax.all_gather(value_output_gradient, "fsdp", axis=0, tiled=True),
        value_frozen_weight,
        (((1,), (1,)), ((), ())),
        preferred_element_type=jnp.float32,
    ).astype(jnp.bfloat16)
    passed_gradient = lax.all_to_all(columns, "fsdp", split_axis=0, concat_axis=1, tiled=True)
    layer_input_gradient, down_term, up_term = decoder_layer_block(
        hidden,
        residual_gradient,
        value_output_gradient,
        attention_norm_gain,
        passed_gradient,
        value_down_factor,
        value_up_factor,
    )
    member = lax.axis_index(("fsdp", "enc"))
    local_images = image_first_rows.shape[0]
    local_counts = lax.dynamic_slice_in_dim(
        image_token_counts, member * local_images, local_images, 0
    )
    slots_out = take_slots(layer_input_gradient, local_counts, image_first_rows)
    received = lax.all_to_all(slots_out, ("fsdp", "enc"), split_axis=1, concat_axis=0, tiled=True)
    source, valid_rows = owner_layout(
        image_token_counts, image_encoder_owner, owner_count, owner_room, MAXIMG
    )
    visual_tokens = jnp.where(
        valid_rows[:, None], jnp.take(received, source, axis=0), jnp.zeros((), received.dtype)
    )
    value_partial_sum = lax.dot_general(
        visual_tokens,
        merger_frozen_weight,
        (((1,), (1,)), ((), ())),
        preferred_element_type=jnp.float32,
    )
    low_part = lax.dot_general(
        visual_tokens,
        merger_up_factor,
        (((1,), (1,)), ((), ())),
        preferred_element_type=jnp.float32,
    )
    value_partial_sum = value_partial_sum + adapter_scale * jnp.dot(
        low_part, merger_down_factor.astype(jnp.float32).T, precision=lax.Precision.HIGHEST
    )
    combined_gradient, low_sum = (
        lax.psum_scatter(value_partial_sum, ("fsdp", "enc"), scatter_dimension=0, tiled=True),
        lax.psum_scatter(low_part, ("fsdp", "enc"), scatter_dimension=0, tiled=True),
    )
    preactivation_gradient = (combined_gradient * (normal_cdf + preact * normal_pdf)).astype(
        jnp.bfloat16
    )
    term_a2 = lax.dot_general(
        activation,
        low_sum.astype(jnp.bfloat16),
        (((0,), (0,)), ((), ())),
        preferred_element_type=jnp.float32,
    )
    term_b2 = lax.dot_general(
        all_low, visual_tokens, (((0,), (0,)), ((), ())), preferred_element_type=jnp.float32
    )
    merger_up_gradient = lax.psum(scale_factor * term_b2, "dp")
    value_down_gradient, value_up_gradient, merger_down_gradient = lax.psum(
        (scale_factor * down_term, scale_factor * up_term, scale_factor * term_a2),
        ("dp", "fsdp", "enc"),
    )
    return (
        layer_input_gradient,
        preactivation_gradient,
        value_down_gradient,
        value_up_gradient,
        merger_down_gradient,
        merger_up_gradient,
    )


def solution(mesh):
    placed = (
        P(("dp", "fsdp", "enc"), None),
        P(("dp", "fsdp", "enc"), None),
        P(("dp", "fsdp", "enc"), None),
        P(),
        P("fsdp", None),
        P(),
        P(),
        P(None, ("fsdp", "enc")),
        P(),
        P(None, ("fsdp", "enc")),
        P(("dp", "fsdp", "enc"), None),
        P("dp"),
        P("dp"),
        P(("dp", "fsdp", "enc")),
    )
    return jax.shard_map(
        body,
        mesh=mesh,
        in_specs=placed,
        out_specs=(
            P(("dp", "fsdp", "enc"), None),
            P(("dp", "fsdp", "enc"), None),
            P(),
            P(),
            P(),
            P(None, ("fsdp", "enc")),
        ),
        check_vma=False,
    )
```

profile of v0, /device:TPU:0, one launch (start us, length us, event | category | flops | bytes accessed | tf_op | source)
XLA Modules:
  0.0 520.8 jit_solution(2232127266080886779)
XLA Ops:
  7.9 25.7 %all-gather.3.cloned.1.call-done = bf16[512,1024]{1,0:T(8,128)(2,1)} async-done(((bf16[256,1024]{1,0:T(8,128)(2,1)}), bf16[512,1024]{1,0:T(8,128)(2,1)}) %all-gather.3.cloned.1.call-update) | async-done | bytes 1048592 | tf_op jit(solution)/shard_map/all_gather | solution.py:121
  33.6 10.3 %convolution_convert_fusion = bf16[512,4096]{1,0:T(8,128)(2,1)} fusion(bf16[512,1024]{1,0:T(8,128)(2,1)} %all-gather.3.cloned.1.call-done, bf16[4096,1024]{1,0:T(8,128)(2,1)} %param.18), kind=kOutput, calls=%fused_computation.19 | convolution fusion | flops 4297064448 | bytes 13631488 | tf_op jit(solution)/shard_map/dot_general | solution.py:120
  43.9 5.7 %all-to-all-start = ((bf16[2,256,4096]{2,1,0:T(8,128)(2,1)}), bf16[2,256,4096]{2,1,0:T(8,128)(2,1)}, u32[]{:S(2)}, u32[]{:S(2)}) async-start(bf16[2,256,4096]{2,1,0:T(8,128)(2,1)} %bitcast.45), calls=%async_computation | async-start | bytes 8388608 | tf_op jit(solution)/shard_map/all_to_all | solution.py:126
  52.1 45.0 %all-to-all-done = bf16[2,256,4096]{2,1,0:T(8,128)(2,1)} async-done(((bf16[2,256,4096]{2,1,0:T(8,128)(2,1)}), bf16[2,256,4096]{2,1,0:T(8,128)(2,1)}, u32[]{:S(2)}, u32[]{:S(2)}) %all-to-all-start) | async-done | bytes 4194336 | tf_op jit(solution)/shard_map/all_to_all | solution.py:126
  97.1 3.3 convert_bitcast_fusion
  102.6 2.9 fusion.2
  105.5 3.5 fusion.5
  109.0 2.0 copy-done.2
  111.9 4.6 all-to-all-start.1
  116.8 8.6 %all-to-all-done.1 = bf16[16,8,1024]{2,0,1:T(8,128)(2,1)S(1)} async-done(((bf16[16,8,1024]{2,0,1:T(8,128)(2,1)}), bf16[16,8,1024]{2,0,1:T(8,128)(2,1)S(1)}, u32[]{:S(2)}, u32[]{:S(2)}) %all-to-all-start.1) | async-done | bytes 262176 | tf_op jit(solution)/shard_map/all_to_all | solution.py:142
  127.0 12.6 %fusion.37 = f32[256,5120]{1,0:T(8,128)} fusion(bf16[256,1024]{1,0:T(8,128)(2,1)S(1)} %select_select_fusion, bf16[5120,1024]{1,0:T(8,128)(2,1)} %param.21), kind=kOutput, calls=%fused_computation.69 | convolution fusion | flops 2684354560 | bytes 16252928 | tf_op jit(solution)/shard_map/dot_general | solution.py:149
  140.5 7.2 %fusion.9 = f32[256,5120]{1,0:T(8,128)} fusion(f32[256,5120]{1,0:T(8,128)} %fusion.37, f32[256,16]{0,1:T(8,128)S(1)} %fusion.38, bf16[5120,16]{0,1:T(8,128)(2,1)S(1)} %copy-done.6), kind=kOutput, calls=%fused_computation.18 | convolution fusion | flops 254279680 | bytes 10665984 | tf_op jit(solution)/shard_map/dot_general | solution.py:161
  147.7 4.2 convolution_multiply_fusion.1
  151.9 4.4 convolution_multiply_fusion.5
  156.3 43.3 %reduce-scatter.7.cloned.1.call-done = f32[32,16]{1,0:T(8,128)} async-done(((f32[256,16]{1,0:T(8,128)}), f32[32,16]{1,0:T(8,128)}) %reduce-scatter.7.cloned.1.call-update) | async-done | bytes 2064
  200.4 104.9 %reduce-scatter.5.cloned.1.call-done = f32[32,5120]{1,0:T(8,128)} async-done(((f32[256,5120]{1,0:T(8,128)}), f32[32,5120]{1,0:T(8,128)}) %reduce-scatter.5.cloned.1.call-update) | async-done | bytes 655376 | tf_op jit(solution)/shard_map/reduce_scatter | solution.py:165
  305.3 2.1 fusion.26
  307.6 30.6 %all-gather = bf16[8,32,16]{1,2,0:T(8,128)(2,1)S(1)} all-gather(bf16[1,32,16]{1,2,0:T(8,128)(2,1)S(1)} %fusion.18), channel_id=1, replica_groups=mesh['dp'=4,'fsdp'=2,'enc'=4] {'fsdp','enc'}, dimensions={0}, use_global_device_ids=true | all-gather | bytes 9216 | tf_op jit(solution)/shard_map/all_gather | solution.py:119
  340.2 30.3 %all-reduce.5.cloned.1.call-done = f32[16,1024]{1,0:T(8,128)} async-done(((f32[16,1024]{1,0:T(8,128)}), f32[16,1024]{1,0:T(8,128)}) %all-reduce.5.cloned.1.call-update) | async-done | bytes 65552 | tf_op jit(solution)/shard_map/psum | solution.py:180
  370.5 137.3 %all-reduce.7.cloned.1.call-done = (f32[8192,16]{0,1:T(8,128)}, f32[16,1024]{1,0:T(8,128)}, f32[5120,16]{0,1:T(8,128)}) async-done(((f32[8192,16]{0,1:T(8,128)}, f32[16,1024]{1,0:T(8,128)}, f32[5120,16]{0,1:T(8,128)}), (f32[8192,16]{0,1:T(8,128)}, f32[16,1024]{1,0:T(8,128)}, f32[5120,16]{0,1:T(8,128)})) %all-reduce.7.cloned.1.call-update) | async-done | bytes 917520 | tf_op jit(solution)/shard_map/psum | solution.py:181
  507.7 1.9 copy.42
  509.6 1.5 copy.43
  511.1 1.7 copy.44
  512.8 1.5 copy.45
  (59 shorter events, 11.2 us)
Async XLA Ops:
  7.2 94.2 %copy-start = (bf16[8192,16]{0,1:T(8,128)(2,1)S(1)}, bf16[8192,16]{0,1:T(8,128)(2,1)}, u32[]{:S(2)}) copy-start(bf16[8192,16]{0,1:T(8,128)(2,1)} %param.19) | copy-start | bytes 786436
  7.2 26.4 %all-gather.3.cloned.1.call-start = ((), (), s32[]{:S(2)}) async-start(), calls=%async_computation.4 | async-start | bytes 1572864 | tf_op jit(solution)/shard_map/all_gather | solution.py:121
  43.8 6.4 %copy-start.11 = (s32[8]{0:T(128)S(1)}, s32[8]{0:T(128)}, u32[]{:S(2)}) copy-start(s32[8]{0:T(128)} %param.25) | copy-start | bytes 100
  43.9 7.0 %copy-start.10 = (s32[8]{0:T(128)S(1)}, s32[8]{0:T(128)}, u32[]{:S(2)}) copy-start(s32[8]{0:T(128)} %param.26) | copy-start | bytes 100
  43.9 8.0 %copy-start.5 = (bf16[256,1024]{1,0:T(8,128)(2,1)S(1)}, bf16[256,1024]{1,0:T(8,128)(2,1)}, u32[]{:S(2)}) copy-start(bf16[256,1024]{1,0:T(8,128)(2,1)} %param.16) | copy-start | bytes 1572868
  43.9 8.0 %copy-start.8 = (bf16[16,1024]{1,0:T(8,128)(2,1)S(1)}, bf16[16,1024]{1,0:T(8,128)(2,1)}, u32[]{:S(2)}) copy-start(bf16[16,1024]{1,0:T(8,128)(2,1)} %param.20) | copy-start | bytes 98308
  43.9 53.3 %all-to-all-start = ((bf16[2,256,4096]{2,1,0:T(8,128)(2,1)}), bf16[2,256,4096]{2,1,0:T(8,128)(2,1)}, u32[]{:S(2)}, u32[]{:S(2)}) async-start(bf16[2,256,4096]{2,1,0:T(8,128)(2,1)} %bitcast.45), calls=%async_computation | async-start | bytes 8388608 | tf_op jit(solution)/shard_map/all_to_all | solution.py:126
  100.4 2.2 copy-start.1
  100.4 2.2 copy-start.7
  102.6 2.9 copy-start.3
  109.0 2.0 copy-start.2
  111.0 15.7 %copy-start.9 = (bf16[16,1024]{1,0:T(8,128)(2,1)S(1)}, bf16[16,1024]{1,0:T(8,128)(2,1)}, u32[]{:S(2)}) copy-start(bf16[16,1024]{1,0:T(8,128)(2,1)} %param.23) | copy-start | bytes 98308
  111.9 13.6 %all-to-all-start.1 = ((bf16[16,8,1024]{2,0,1:T(8,128)(2,1)}), bf16[16,8,1024]{2,0,1:T(8,128)(2,1)S(1)}, u32[]{:S(2)}, u32[]{:S(2)}) async-start(bf16[16,8,1024]{2,0,1:T(8,128)(2,1)} %bitcast.39), calls=%async_computation.1 | async-start | bytes 524288 | tf_op jit(solution)/shard_map/all_to_all | solution.py:142
  116.5 83.1 %reduce-scatter.7.cloned.1.call-start = ((), (), s32[]{:S(2)}) async-start(), calls=%async_computation.7 | async-start | bytes 147456
  127.0 13.4 %copy-start.6 = (bf16[5120,16]{0,1:T(8,128)(2,1)S(1)}, bf16[5120,16]{0,1:T(8,128)(2,1)}, u32[]{:S(2)}) copy-start(bf16[5120,16]{0,1:T(8,128)(2,1)} %param.22) | copy-start | bytes 491524
  140.4 164.9 %reduce-scatter.5.cloned.1.call-start = ((), (), s32[]{:S(2)}) async-start(), calls=%async_computation.5 | async-start | bytes 5898240 | tf_op jit(solution)/shard_map/reduce_scatter | solution.py:165
  147.7 157.6 %copy-start.4 = (bf16[32,5120]{1,0:T(8,128)(2,1)S(1)}, bf16[32,5120]{1,0:T(8,128)(2,1)}, u32[]{:S(2)}) copy-start(bf16[32,5120]{1,0:T(8,128)(2,1)} %param.24) | copy-start | bytes 983044
  147.7 222.8 %all-reduce.5.cloned.1.call-start = ((), (), s32[]{:S(2)}) async-start(), calls=%async_computation.6 | async-start | bytes 131072 | tf_op jit(solution)/shard_map/psum | solution.py:180
  339.2 168.6 %all-reduce.7.cloned.1.call-start = ((), (), s32[]{:S(2)}) async-start(), calls=%async_computation.8 | async-start | bytes 1835008 | tf_op jit(solution)/shard_map/psum | solution.py:181
Sparse Core Ops, SparseCore 0:
  9.5 23.9 all-gather.2
  140.5 59.0 reduce-scatter.6
  203.2 102.0 reduce-scatter.4
  339.3 31.1 all-reduce.4
  376.4 131.3 all-reduce.6
where the time goes:
time: 522 us; the launch traced here: 521 us
  waiting for transfers between devices  396 us (76%)
  matrix products  44 us (8%)
  blocking collectives  30.6 us (6%)
  local copies, waits for them, and re-layouts  14.9 us (3%)
  between operations  14.6 us (3%)
  starting transfers between devices  10.7 us (2%)
  other arithmetic  10.2 us (2%)
    psum x1, waiting for transfers between devices, body(): lax.psum((scale_factor * down_term, scale_factor * up_term, scale_factor...  137 us
    reduce_scatter x1, waiting for transfers between devices, body(): lax.psum_scatter(value_partial_sum, ('fsdp', 'enc'), scatter_dimension=0,...  105 us
    all_to_all x1, waiting for transfers between devices, body(): lax.all_to_all(columns, 'fsdp', split_axis=0, concat_axis=1, tiled=True)  45 us
    unnamed x6, waiting for transfers between devices  44.1 us
    all_gather x1, blocking collectives, body(): all_low = lax.all_gather(act_low, ('fsdp', 'enc'), axis=0, tiled=True)  30.6 us
    psum x1, waiting for transfers between devices, body(): merger_up_gradient = lax.psum(scale_factor * term_b2, 'dp')  30.3 us
    all_gather x1, waiting for transfers between devices, body(): lax.all_gather(value_output_gradient, 'fsdp', axis=0, tiled=True)  25.7 us
    dot_general x1, matrix products, body(): lax.dot_general(visual_tokens, merger_frozen_weight, (((1,), (1,)), ((),...  12.6 us
  transfers between devices with their start and end apart: 7, of which 7 were waited for; matrix products, arithmetic and copies ran while one was open for 4% of the time, Pallas kernels for 0%

commit v1 on v0

--- a/solution.py
+++ b/solution.py
@@ -123,7 +123,10 @@
         (((1,), (1,)), ((), ())),
         preferred_element_type=jnp.float32,
     ).astype(jnp.bfloat16)
-    passed_gradient = lax.all_to_all(columns, "fsdp", split_axis=0, concat_axis=1, tiled=True)
+    passed_gradient = jnp.concatenate(
+        lax.all_to_all(jnp.stack(jnp.split(columns, lax.axis_size("fsdp"), axis=0)), "fsdp", 0, 0),
+        axis=1,
+    )
     layer_input_gradient, down_term, up_term = decoder_layer_block(
         hidden,
         residual_gradient,

time: 522 us -> 545 us (1.044)
  local copies, waits for them, and re-layouts: 14.9 us -> 31.9 us
    convert_element_type x1 -> x2, local copies, waits for them, and re-layouts: 0.98 us -> 17.8 us  [decoder_layer_block(): passed_gradient.astype(jnp.float32)]
    convert_element_type x0 -> x1, other arithmetic: none -> 6.49 us  [decoder_layer_block(): passed_gradient.astype(jnp.float32)]
where the time goes in v1:
time: 545 us; the launch traced here: 544 us
  waiting for transfers between devices  396 us (73%)
  matrix products  45.2 us (8%)
  local copies, waits for them, and re-layouts  31.9 us (6%)
  blocking collectives  30.6 us (6%)
  other arithmetic  15.6 us (3%)
  between operations  14.7 us (3%)
  starting transfers between devices  10.6 us (2%)
    psum x1, waiting for transfers between devices, body(): lax.psum((scale_factor * down_term, scale_factor * up_term, scale_factor...  137 us
    reduce_scatter x1, waiting for transfers between devices, body(): lax.psum_scatter(value_partial_sum, ('fsdp', 'enc'), scatter_dimension=0,...  105 us
    all_to_all x1, waiting for transfers between devices, body(): lax.all_to_all(jnp.stack(jnp.split(columns, lax.axis_size('fsdp'), axis=0...  45 us
    unnamed x6, waiting for transfers between devices  44.1 us
    all_gather x1, blocking collectives, body(): all_low = lax.all_gather(act_low, ('fsdp', 'enc'), axis=0, tiled=True)  30.6 us
    psum x1, waiting for transfers between devices, body(): merger_up_gradient = lax.psum(scale_factor * term_b2, 'dp')  30.3 us
    all_gather x1, waiting for transfers between devices, body(): lax.all_gather(value_output_gradient, 'fsdp', axis=0, tiled=True)  25.7 us
    convert_element_type x2, local copies, waits for them, and re-layouts, decoder_layer_block(): passed_gradient.astype(jnp.float32)  17.8 us
  transfers between devices with their start and end apart: 7, of which 7 were waited for; matrix products, arithmetic and copies ran while one was open for 4% of the time, Pallas kernels for 0%

profile of v1, /device:TPU:0, one launch (start us, length us, event | category | flops | bytes accessed | tf_op | source)
XLA Modules:
  0.0 544.4 jit_solution(10508949690327402606)
XLA Ops:
  7.9 25.7 %all-gather.3.cloned.1.call-done = bf16[512,1024]{1,0:T(8,128)(2,1)} async-done(((bf16[256,1024]{1,0:T(8,128)(2,1)}), bf16[512,1024]{1,0:T(8,128)(2,1)}) %all-gather.3.cloned.1.call-update) | async-done | bytes 1048592 | tf_op jit(solution)/shard_map/all_gather | solution.py:121
  33.6 8.3 %convolution_convert_fusion = bf16[512,4096]{1,0:T(8,128)(2,1)S(1)} fusion(bf16[512,1024]{1,0:T(8,128)(2,1)} %all-gather.3.cloned.1.call-done, bf16[4096,1024]{1,0:T(8,128)(2,1)} %param.18), kind=kOutput, calls=%fused_computation.19 | convolution fusion | flops 4297064448 | bytes 13631488 | tf_op jit(solution)/shard_map/dot_general | solution.py:120
  42.4 2.4 pad_maximum_fusion
  44.8 5.6 %all-to-all-start = ((bf16[2,256,4096]{2,1,0:T(8,128)(2,1)}), bf16[2,256,4096]{2,1,0:T(8,128)(2,1)}, u32[]{:S(2)}, u32[]{:S(2)}) async-start(bf16[2,256,4096]{2,1,0:T(8,128)(2,1)} %pad_maximum_fusion), calls=%async_computation | async-start | bytes 8388608 | tf_op jit(solution)/shard_map/all_to_all | solution.py:127
  52.9 45.0 %all-to-all-done = bf16[2,256,4096]{2,1,0:T(8,128)(2,1)} async-done(((bf16[2,256,4096]{2,1,0:T(8,128)(2,1)}), bf16[2,256,4096]{2,1,0:T(8,128)(2,1)}, u32[]{:S(2)}, u32[]{:S(2)}) %all-to-all-start) | async-done | bytes 4194336 | tf_op jit(solution)/shard_map/all_to_all | solution.py:127
  97.9 6.5 %convert_bitcast_fusion = f32[256,2,4096]{2,0,1:T(8,128)} fusion(bf16[2,256,4096]{2,1,0:T(8,128)(2,1)} %all-to-all-done), kind=kLoop, calls=%fused_computation.16 | loop fusion | flops 2097152 | bytes 12582912 | tf_op jit(solution)/shard_map/convert_element_type | solution.py:68
  104.4 8.9 %copy.29 = f32[256,2,4096]{0,2,1:T(8,128)} copy(f32[256,2,4096]{2,0,1:T(8,128)} %convert_bitcast_fusion) | data formatting | bytes 16777216 | tf_op jit(solution)/shard_map/convert_element_type | solution.py:68
  113.3 8.9 %copy.30 = f32[256,8192]{1,0:T(8,128)} copy(f32[256,8192]{0,1:T(8,128)} %bitcast.46) | data formatting | bytes 16777216 | tf_op jit(solution)/shard_map/convert_element_type | solution.py:68
  122.2 6.2 %fusion.2 = (f32[256]{0:T(256)S(1)}, f32[256]{0:T(256)S(1)}, f32[256,8192]{1,0:T(8,128)S(1)}) fusion(bf16[256,8192]{1,0:T(8,128)(2,1)} %param.14, f32[256,8192]{1,0:T(8,128)} %copy.30, bf16[256,16]{0,1:T(8,128)(2,1)S(1)} %convolution_convert_fusion.1, bf16[8192,16]{0,1:T(8,128)(2,1)S(1)} %copy-done, f32[8192]{0:T(1024)S(1)} %copy-done.7), kind=kOutput, calls=%fused_computation.9 | convolution fusion | flops 83885568 | bytes 21276672 | tf_op jit(solution)/shard_map/dot_general | solution.py:68
  129.3 3.3 fusion.5
  132.7 2.0 copy-done.2
  135.5 4.6 all-to-all-start.1
  140.5 8.6 %all-to-all-done.1 = bf16[16,8,1024]{2,0,1:T(8,128)(2,1)S(1)} async-done(((bf16[16,8,1024]{2,0,1:T(8,128)(2,1)}), bf16[16,8,1024]{2,0,1:T(8,128)(2,1)S(1)}, u32[]{:S(2)}, u32[]{:S(2)}) %all-to-all-start.1) | async-done | bytes 262176 | tf_op jit(solution)/shard_map/all_to_all | solution.py:145
  150.7 12.6 %fusion.37 = f32[256,5120]{1,0:T(8,128)} fusion(bf16[256,1024]{1,0:T(8,128)(2,1)S(1)} %select_select_fusion, bf16[5120,1024]{1,0:T(8,128)(2,1)} %param.21), kind=kOutput, calls=%fused_computation.72 | convolution fusion | flops 2684354560 | bytes 16252928 | tf_op jit(solution)/shard_map/dot_general | solution.py:152
  164.1 7.2 %fusion.9 = f32[256,5120]{1,0:T(8,128)} fusion(f32[256,5120]{1,0:T(8,128)} %fusion.37, f32[256,16]{0,1:T(8,128)S(1)} %fusion.38, bf16[5120,16]{0,1:T(8,128)(2,1)S(1)} %copy-done.6), kind=kOutput, calls=%fused_computation.18 | convolution fusion | flops 254279680 | bytes 10665984 | tf_op jit(solution)/shard_map/dot_general | solution.py:164
  171.3 4.2 convolution_multiply_fusion.1
  175.5 4.4 convolution_multiply_fusion.5
  179.9 43.3 %reduce-scatter.7.cloned.1.call-done = f32[32,16]{1,0:T(8,128)} async-done(((f32[256,16]{1,0:T(8,128)}), f32[32,16]{1,0:T(8,128)}) %reduce-scatter.7.cloned.1.call-update) | async-done | bytes 2064
  224.1 104.8 %reduce-scatter.5.cloned.1.call-done = f32[32,5120]{1,0:T(8,128)} async-done(((f32[256,5120]{1,0:T(8,128)}), f32[32,5120]{1,0:T(8,128)}) %reduce-scatter.5.cloned.1.call-update) | async-done | bytes 655376 | tf_op jit(solution)/shard_map/reduce_scatter | solution.py:168
  328.9 2.1 fusion.26
  331.2 30.6 %all-gather = bf16[8,32,16]{1,2,0:T(8,128)(2,1)S(1)} all-gather(bf16[1,32,16]{1,2,0:T(8,128)(2,1)S(1)} %fusion.18), channel_id=1, replica_groups=mesh['dp'=4,'fsdp'=2,'enc'=4] {'fsdp','enc'}, dimensions={0}, use_global_device_ids=true | all-gather | bytes 9216 | tf_op jit(solution)/shard_map/all_gather | solution.py:119
  363.8 30.3 %all-reduce.5.cloned.1.call-done = f32[16,1024]{1,0:T(8,128)} async-done(((f32[16,1024]{1,0:T(8,128)}), f32[16,1024]{1,0:T(8,128)}) %all-reduce.5.cloned.1.call-update) | async-done | bytes 65552 | tf_op jit(solution)/shard_map/psum | solution.py:183
  394.1 137.3 %all-reduce.7.cloned.1.call-done = (f32[8192,16]{0,1:T(8,128)}, f32[16,1024]{1,0:T(8,128)}, f32[5120,16]{0,1:T(8,128)}) async-done(((f32[8192,16]{0,1:T(8,128)}, f32[16,1024]{1,0:T(8,128)}, f32[5120,16]{0,1:T(8,128)}), (f32[8192,16]{0,1:T(8,128)}, f32[16,1024]{1,0:T(8,128)}, f32[5120,16]{0,1:T(8,128)})) %all-reduce.7.cloned.1.call-update) | async-done | bytes 917520 | tf_op jit(solution)/shard_map/psum | solution.py:184
  531.4 1.9 copy.43
  (62 shorter events, 15.0 us)
Async XLA Ops:
  7.2 115.0 %copy-start = (bf16[8192,16]{0,1:T(8,128)(2,1)S(1)}, bf16[8192,16]{0,1:T(8,128)(2,1)}, u32[]{:S(2)}) copy-start(bf16[8192,16]{0,1:T(8,128)(2,1)} %param.19) | copy-start | bytes 786436
  7.2 26.4 %all-gather.3.cloned.1.call-start = ((), (), s32[]{:S(2)}) async-start(), calls=%async_computation.4 | async-start | bytes 1572864 | tf_op jit(solution)/shard_map/all_gather | solution.py:121
  42.3 8.7 %copy-start.11 = (s32[8]{0:T(128)S(1)}, s32[8]{0:T(128)}, u32[]{:S(2)}) copy-start(s32[8]{0:T(128)} %param.25) | copy-start | bytes 100
  42.3 9.3 %copy-start.10 = (s32[8]{0:T(128)S(1)}, s32[8]{0:T(128)}, u32[]{:S(2)}) copy-start(s32[8]{0:T(128)} %param.26) | copy-start | bytes 100
  42.4 10.3 %copy-start.5 = (bf16[256,1024]{1,0:T(8,128)(2,1)S(1)}, bf16[256,1024]{1,0:T(8,128)(2,1)}, u32[]{:S(2)}) copy-start(bf16[256,1024]{1,0:T(8,128)(2,1)} %param.16) | copy-start | bytes 1572868
  42.4 10.3 %copy-start.8 = (bf16[16,1024]{1,0:T(8,128)(2,1)S(1)}, bf16[16,1024]{1,0:T(8,128)(2,1)}, u32[]{:S(2)}) copy-start(bf16[16,1024]{1,0:T(8,128)(2,1)} %param.20) | copy-start | bytes 98308
  44.8 53.1 %all-to-all-start = ((bf16[2,256,4096]{2,1,0:T(8,128)(2,1)}), bf16[2,256,4096]{2,1,0:T(8,128)(2,1)}, u32[]{:S(2)}, u32[]{:S(2)}) async-start(bf16[2,256,4096]{2,1,0:T(8,128)(2,1)} %pad_maximum_fusion), calls=%async_computation | async-start | bytes 8388608 | tf_op jit(solution)/shard_map/all_to_all | solution.py:127
  113.3 8.9 %copy-start.7 = (f32[8192]{0:T(1024)S(1)}, f32[8192]{0:T(1024)}, u32[]{:S(2)}) copy-start(f32[8192]{0:T(1024)} %param.17) | copy-start | bytes 98308
  122.2 6.2 %copy-start.1 = (bf16[256,8192]{1,0:T(8,128)(2,1)S(1)}, bf16[256,8192]{1,0:T(8,128)(2,1)}, u32[]{:S(2)}) copy-start(bf16[256,8192]{1,0:T(8,128)(2,1)} %param.14) | copy-start | bytes 12582916
  122.2 7.1 %copy-start.3 = (bf16[256,8192]{1,0:T(8,128)(2,1)S(1)}, bf16[256,8192]{1,0:T(8,128)(2,1)}, u32[]{:S(2)}) copy-start(bf16[256,8192]{1,0:T(8,128)(2,1)} %param.15) | copy-start | bytes 12582916
  132.7 2.0 copy-start.2
  134.7 15.7 %copy-start.9 = (bf16[16,1024]{1,0:T(8,128)(2,1)S(1)}, bf16[16,1024]{1,0:T(8,128)(2,1)}, u32[]{:S(2)}) copy-start(bf16[16,1024]{1,0:T(8,128)(2,1)} %param.23) | copy-start | bytes 98308
  135.5 13.6 %all-to-all-start.1 = ((bf16[16,8,1024]{2,0,1:T(8,128)(2,1)}), bf16[16,8,1024]{2,0,1:T(8,128)(2,1)S(1)}, u32[]{:S(2)}, u32[]{:S(2)}) async-start(bf16[16,8,1024]{2,0,1:T(8,128)(2,1)} %bitcast.41), calls=%async_computation.1 | async-start | bytes 524288 | tf_op jit(solution)/shard_map/all_to_all | solution.py:145
  140.1 83.1 %reduce-scatter.7.cloned.1.call-start = ((), (), s32[]{:S(2)}) async-start(), calls=%async_computation.7 | async-start | bytes 147456
  150.7 13.4 %copy-start.6 = (bf16[5120,16]{0,1:T(8,128)(2,1)S(1)}, bf16[5120,16]{0,1:T(8,128)(2,1)}, u32[]{:S(2)}) copy-start(bf16[5120,16]{0,1:T(8,128)(2,1)} %param.22) | copy-start | bytes 491524
  164.0 164.9 %reduce-scatter.5.cloned.1.call-start = ((), (), s32[]{:S(2)}) async-start(), calls=%async_computation.5 | async-start | bytes 5898240 | tf_op jit(solution)/shard_map/reduce_scatter | solution.py:168
  171.3 157.6 %copy-start.4 = (bf16[32,5120]{1,0:T(8,128)(2,1)S(1)}, bf16[32,5120]{1,0:T(8,128)(2,1)}, u32[]{:S(2)}) copy-start(bf16[32,5120]{1,0:T(8,128)(2,1)} %param.24) | copy-start | bytes 983044
  171.3 222.8 %all-reduce.5.cloned.1.call-start = ((), (), s32[]{:S(2)}) async-start(), calls=%async_computation.6 | async-start | bytes 131072 | tf_op jit(solution)/shard_map/psum | solution.py:183
  362.8 168.6 %all-reduce.7.cloned.1.call-start = ((), (), s32[]{:S(2)}) async-start(), calls=%async_computation.8 | async-start | bytes 1835008 | tf_op jit(solution)/shard_map/psum | solution.py:184
Sparse Core Ops, SparseCore 0:
  9.5 23.9 all-gather.2
  164.2 59.0 reduce-scatter.6
  226.9 102.0 reduce-scatter.4
  362.9 31.1 all-reduce.4
  400.0 131.3 all-reduce.6
